TPU v7x, 512 devices: a whole 4x8x8 slice. The times are simulated.
512 devices in a mesh: plane: 32 (over x, z), tile: 16 (over y, core).
Axes of the slice: x: 4, y: 8, z: 8, core: 2. Of those that a mesh axis runs over, the one named last changes fastest.
Arguments:
- raw_planes: bfloat16 [3072, 512, 512], P('plane', 'tile'), may hold values from -6 to 6
- pair_sections: int32 [2048, 2], P('plane'), may hold values from 0 to 47
- pair_rows: int32 [2048, 2], P('plane'), may hold values from 0 to 128
- pair_extent: int32 [2048], P('plane'), may hold values from 64 to 128
- pair_owner: int32 [2048, 1], P('plane'), may hold values from 0 to 15; in each aligned block of 64 rows (0 to 63, 64 to 127, ...) at most 12 rows name the same one
Outputs:
- surface_out: bfloat16 [6144, 128, 256], P(('plane', 'tile'))
Inputs may be any that keep to these rules, and one draw needn't show every extreme that they name: `pair_owner`: among the 64 pairs of one slab no owner takes more than 12 pairs.
All inputs are finite; a program needn't handle non-finite values.
Results may differ from a plain program's by a relative error of at most 0.012.
The roundings to bfloat16 on the way count: a program that leaves them out, or rounds other values in their place, can miss the bound.
Values may be sent and summed in bfloat16 or wider, within the bound.
No kernel may reach another device: no remote copies, remote signals or barrier semaphores. Data moves between devices by JAX's collectives and lax.ppermute only.
A program may use at most 64 MiB of HBM per device.

v0:
```python
import math
import jax
import jax.numpy as jnp
from jax import lax
from jax.sharding import PartitionSpec as P

BAND = 128
OWN_CAP = 12


def from_behind(value, axis, steps):
    count = lax.axis_size(axis)
    initial, last = (max(0, -steps), min(count, count - steps))
    return lax.ppermute(value, axis, [(source, source + steps) for source in range(initial, last)])


def blur_matrix(face_cells, half_cells):
    source = jnp.arange(face_cells, dtype=jnp.int32)[:, None]
    target = jnp.arange(half_cells, dtype=jnp.int32)[None, :]
    offset = jnp.abs(source - 2 * target)
    weights = jnp.where(
        offset == 0, 6.0, jnp.where(offset == 1, 4.0, jnp.where(offset == 2, 1.0, 0.0))
    )
    return (weights * 0.0625).astype(jnp.bfloat16)


def dft_tables(length):
    indices = jnp.arange(length, dtype=jnp.int32)
    phases = indices[:, None] * indices[None, :] % length
    angles = phases.astype(jnp.float32) * (2.0 * math.pi / length)
    factor = 1.0 / math.sqrt(length)
    return (
        (jnp.cos(angles) * factor).astype(jnp.bfloat16),
        (jnp.sin(angles) * factor).astype(jnp.bfloat16),
    )


def correlate(first_bands, second_bands):
    pair_count = first_bands.shape[0]
    band_rows = first_bands.shape[1]
    columns = first_bands.shape[2]
    cos_half, sin_half = dft_tables(columns)
    cos_band, sin_band = dft_tables(band_rows)
    stacked = jnp.concatenate([first_bands, second_bands], axis=0).reshape(
        2 * pair_count * band_rows, columns
    )
    forward_table = jnp.concatenate([cos_half, -sin_half], axis=1)
    rowwise = jnp.dot(stacked, forward_table, preferred_element_type=jnp.float32).astype(
        jnp.bfloat16
    )
    rowwise = rowwise.reshape(2 * pair_count, band_rows, 2 * columns)
    row_real = rowwise[:, :, :columns]
    row_imag = rowwise[:, :, columns:]
    spec_real = jnp.einsum(
        "uv,kvj->kuj", cos_band, row_real, preferred_element_type=jnp.float32
    ) + jnp.einsum("uv,kvj->kuj", sin_band, row_imag, preferred_element_type=jnp.float32)
    spec_imag = jnp.einsum(
        "uv,kvj->kuj", cos_band, row_imag, preferred_element_type=jnp.float32
    ) - jnp.einsum("uv,kvj->kuj", sin_band, row_real, preferred_element_type=jnp.float32)
    first_real = spec_real[:pair_count]
    first_imag = spec_imag[:pair_count]
    second_real = spec_real[pair_count:]
    second_imag = spec_imag[pair_count:]
    cross_real = first_real * second_real + first_imag * second_imag
    cross_imag = first_imag * second_real - first_real * second_imag
    magnitude = jnp.sqrt(cross_real * cross_real + cross_imag * cross_imag)
    mean_level = jnp.mean(magnitude, axis=(1, 2), keepdims=True) + 1e-06
    divisor = magnitude + mean_level
    norm_real = (cross_real / divisor).astype(jnp.bfloat16)
    norm_imag = (cross_imag / divisor).astype(jnp.bfloat16)
    col_real = (
        jnp.einsum("uv,kvj->kuj", cos_band, norm_real, preferred_element_type=jnp.float32)
        - jnp.einsum("uv,kvj->kuj", sin_band, norm_imag, preferred_element_type=jnp.float32)
    ).astype(jnp.bfloat16)
    col_imag = (
        jnp.einsum("uv,kvj->kuj", cos_band, norm_imag, preferred_element_type=jnp.float32)
        + jnp.einsum("uv,kvj->kuj", sin_band, norm_real, preferred_element_type=jnp.float32)
    ).astype(jnp.bfloat16)
    joined = jnp.concatenate([col_real, col_imag], axis=2).reshape(
        pair_count * band_rows, 2 * columns
    )
    inverse_table = jnp.concatenate([cos_half, -sin_half], axis=0)
    surface = jnp.dot(joined, inverse_table, preferred_element_type=jnp.float32)
    return surface.reshape(pair_count, band_rows, columns).astype(jnp.bfloat16)


def fetch_bands(sections, section_ids, first_rows, extents):
    wanted = section_ids.shape[0]
    columns = sections.shape[2]
    zero_index = jnp.zeros((), jnp.int32)
    blank_bands = jnp.zeros((wanted, BAND, columns), sections.dtype)
    band_index = jnp.arange(BAND, dtype=jnp.int32)
    shards = lax.all_gather(sections, "tile", axis=0, tiled=True)
    held = shards.shape[0]
    inside = (section_ids >= 0) & (section_ids < held)
    clipped = jnp.clip(section_ids, 0, held - 1)

    def slice_band(which, row_start):
        return lax.dynamic_slice(shards, (which, row_start, zero_index), (1, BAND, columns))[0]

    cutout = jax.vmap(slice_band)(clipped, first_rows)
    bands = jnp.where(inside[:, None, None], cutout, blank_bands)
    live_rows = band_index[None, :, None] < extents[:, None, None]
    return jnp.where(live_rows, bands, jnp.zeros_like(bands))


def pair_bands(sections, pair_sections, pair_rows, pair_extent, chosen):
    picked_ids = jnp.take(pair_sections, chosen, axis=0)
    picked_rows = jnp.take(pair_rows, chosen, axis=0)
    picked_extent = jnp.take(pair_extent, chosen, axis=0)
    section_ids = jnp.concatenate([picked_ids[:, 0], picked_ids[:, 1]], axis=0)
    first_rows = jnp.concatenate([picked_rows[:, 0], picked_rows[:, 1]], axis=0)
    extents = jnp.concatenate([picked_extent, picked_extent], axis=0)
    bands = fetch_bands(sections, section_ids, first_rows, extents)
    pair_count = chosen.shape[0]
    return (bands[:pair_count], bands[pair_count:])


def depth_blur(planar, carried):
    count = planar.shape[0]
    previous = jnp.concatenate([carried[None], planar[: count - 1]], axis=0)
    return (
        (
            previous[0::2].astype(jnp.float32)
            + 2.0 * planar[0::2].astype(jnp.float32)
            + planar[1::2].astype(jnp.float32)
        )
        * 0.25
    ).astype(jnp.bfloat16)


def per_device(raw_planes, pair_sections, pair_rows, pair_extent, pair_owner):
    tile_count = lax.axis_size("tile")
    face_cells = raw_planes.shape[2]
    half_cells = face_cells // 2
    slab_planes = raw_planes.shape[0]
    planes_dev = slab_planes // tile_count
    blur_table = blur_matrix(face_cells, half_cells)
    regrouped = lax.all_to_all(raw_planes, "tile", split_axis=0, concat_axis=1, tiled=True)
    across = jnp.dot(
        regrouped.reshape(planes_dev * face_cells, face_cells),
        blur_table,
        preferred_element_type=jnp.float32,
    )
    across = across.astype(jnp.bfloat16).reshape(planes_dev, face_cells, half_cells)
    planar = jnp.einsum(
        "ri,zrj->zij", blur_table, across, preferred_element_type=jnp.float32
    ).astype(jnp.bfloat16)
    carried = from_behind(planar[planes_dev - 1], ("plane", "tile"), 1)
    sections = depth_blur(planar, carried)
    my_tile = lax.axis_index("tile")
    owners = pair_owner[:, 0]
    listed = owners.shape[0]
    position = jnp.arange(listed, dtype=jnp.int32)
    earlier = (owners[:, None] == owners[None, :]) & (position[None, :] < position[:, None])
    slot_of = jnp.sum(earlier.astype(jnp.int32), axis=1)
    slot_ids = jnp.arange(OWN_CAP, dtype=jnp.int32)
    picked = (owners[None, :] == my_tile) & (slot_of[None, :] == slot_ids[:, None])
    chosen = jnp.sum(jnp.where(picked, position[None, :], 0), axis=1)
    filled = jnp.any(picked, axis=1)
    first_bands, second_bands = pair_bands(sections, pair_sections, pair_rows, pair_extent, chosen)
    surfaces = correlate(first_bands, second_bands)
    return jnp.where(filled[:, None, None], surfaces, jnp.zeros_like(surfaces))


def solution(mesh):
    return jax.shard_map(
        per_device,
        mesh=mesh,
        in_specs=(
            P("plane", "tile", None),
            P("plane", None),
            P("plane", None),
            P("plane"),
            P("plane", None),
        ),
        out_specs=P(("plane", "tile"), None, None),
        check_vma=False,
    )
```

profile of v0, /device:TPU:1, one launch (start us, length us, event | category | flops | bytes accessed | tf_op | source)
XLA Modules:
  0.0 185.8 jit_solution(15391342763990343113)
XLA Ops:
  6.5 0.0 copy-start
  6.5 10.5 %all-to-all-start = ((bf16[96,32,512]{2,1,0:T(8,128)(2,1)}), bf16[96,32,512]{2,1,0:T(8,128)(2,1)S(1)}, u32[]{:S(2)}, u32[]{:S(2)}) async-start(bf16[96,32,512]{2,1,0:T(8,128)(2,1)} %param.7), calls=%async_computation | async-start | bytes 6291456 | tf_op jit(solution)/shard_map/all_to_all | solution.py:139
  17.0 0.0 all-gather.2.cloned.1.call-start
  17.1 70.9 %all-to-all-done = bf16[96,32,512]{2,1,0:T(8,128)(2,1)S(1)} async-done(((bf16[96,32,512]{2,1,0:T(8,128)(2,1)}), bf16[96,32,512]{2,1,0:T(8,128)(2,1)S(1)}, u32[]{:S(2)}, u32[]{:S(2)}) %all-to-all-start) | async-done | bytes 3145760 | tf_op jit(solution)/shard_map/all_to_all | solution.py:139
  88.0 0.2 copy.46
  88.3 1.2 fusion
  89.5 0.7 copy.47
  90.2 0.8 fusion.15
  91.0 2.5 %collective-permute-start = (bf16[256,256]{0,1:T(8,128)(2,1)S(1)}, bf16[256,256]{0,1:T(8,128)(2,1)S(1)}, u32[]{:S(2)}, u32[]{:S(2)}) collective-permute-start(bf16[256,256]{0,1:T(8,128)(2,1)S(1)} %slice_bitcast_fusion), channel_id=1, source_target_pairs={{0,1},{1,2},{2,3},{3,4},{4,5},{5,6},{6,7},{7,8},{8,9},{9,10},{10,1... | collective-permute-start | bytes 393224 | tf_op jit(solution)/shard_map/ppermute | solution.py:14
  93.5 1.7 collective-permute-done
  95.2 0.1 pad_maximum_fusion
  95.3 0.0 copy-start.1
  95.3 0.0 copy-start.2
  95.3 0.0 copy-start.3
  95.3 0.2 multiply_convert_fusion
  95.5 0.9 copy.49
  96.5 0.0 all-gather.2.cloned.1.call-update
  96.5 0.0 copy-done.1
  96.5 0.1 copy.45
  96.6 0.0 copy-done.2
  96.6 0.1 copy.52
  96.7 0.0 copy-done.3
  96.7 0.2 convert_reduce_fusion
  96.9 0.1 select_reduce_fusion
  97.0 0.0 copy-done
  97.0 0.7 gather_fusion
  97.7 0.6 gather_fusion.2
  98.3 0.6 gather_fusion.3
  98.8 0.1 broadcast_select_fusion.1
  98.9 0.2 slice_reduce_fusion.1
  99.1 0.1 copy.54
  99.2 0.1 copy.53
  99.3 0.1 copy.51
  99.4 0.1 copy.50
  99.5 0.1 pad_add_fusion
  99.5 0.1 compare_and_fusion
  99.6 0.1 fusion.66
  99.7 0.1 fusion.59
  99.8 1.0 fusion.37
  100.8 1.0 multiply_convert_fusion.3
  101.8 0.1 broadcast_bitcast_fusion
  101.9 0.1 fusion.57
  102.0 47.4 %all-gather.2.cloned.1.call-done = bf16[48,256,256]{2,1,0:T(8,128)(2,1)} async-done(((bf16[3,256,256]{2,1,0:T(8,128)(2,1)}), bf16[48,256,256]{2,1,0:T(8,128)(2,1)}) %all-gather.2.cloned.1.call-update) | async-done | bytes 6291472 | tf_op jit(solution)/shard_map/all_gather | solution.py:93
  149.4 9.0 %copy.55 = bf16[48,256,256]{2,0,1:T(8,128)(2,1)} copy(bf16[48,256,256]{2,1,0:T(8,128)(2,1)} %all-gather.2.cloned.1.call-done) | data formatting | bytes 12582912 | tf_op jit(solution)/shard_map/all_gather | solution.py:93
  158.4 7.5 %gather_fusion.1 = bf16[24,128,256]{2,0,1:T(8,128)(2,1)S(1)} fusion(bf16[48,256,256]{2,0,1:T(8,128)(2,1)} %copy.55, s32[24]{0:T(128)S(1)} %fusion.66), kind=kCustom, calls=%fused_computation.3 | custom fusion | bytes 3146016 | tf_op jit(solution)/shard_map/vmap()/gather | solution.py:99
  165.8 0.4 copy.56
  166.2 2.4 %fusion.5 = bf16[3072,256]{1,0:T(8,128)(2,1)S(1)} fusion(bf16[24,128,256]{2,1,0:T(8,128)(2,1)S(1)} %copy.56, pred[3072]{0:T(1024)(128)(4,1)S(1)} %broadcast_bitcast_fusion, pred[3072]{0:T(1024)(128)(4,1)S(1)} %fusion.57), kind=kLoop, calls=%fused_computation.14 | loop fusion | flops 1572864 | bytes 3151872 | tf_op jit(solution)/shard_map/jit(_where)/select_n | solution.py:104
  168.6 1.0 convolution_convert_fusion
  169.6 0.8 fusion.10
  170.5 0.8 fusion.12
  171.3 0.8 subtract_bitcast_fusion
  172.1 0.9 add_bitcast_fusion
  173.0 1.2 fusion.21
  174.1 0.8 divide_convert_fusion.1
  175.0 0.6 fusion.50
  175.6 0.6 fusion.52
  176.2 0.6 fusion.17
  176.8 0.6 fusion.16
  177.4 1.5 fusion.18
  (9 shorter events, 0.1 us)
Async XLA Ops:
  6.5 90.5 %copy-start = (s32[64]{0:T(128)S(1)}, s32[64]{0:T(128)}, u32[]{:S(2)}) copy-start(s32[64]{0:T(128)} %param.10) | copy-start | bytes 772
  6.5 81.5 %all-to-all-start = ((bf16[96,32,512]{2,1,0:T(8,128)(2,1)}), bf16[96,32,512]{2,1,0:T(8,128)(2,1)S(1)}, u32[]{:S(2)}, u32[]{:S(2)}) async-start(bf16[96,32,512]{2,1,0:T(8,128)(2,1)} %param.7), calls=%async_computation | async-start | bytes 6291456 | tf_op jit(solution)/shard_map/all_to_all | solution.py:139
  17.0 132.3 %all-gather.2.cloned.1.call-start = ((), (), s32[]{:S(2)}) async-start(), calls=%async_computation.1 | async-start | bytes 6684672 | tf_op jit(solution)/shard_map/all_gather | solution.py:93
  91.0 4.2 %collective-permute-start = (bf16[256,256]{0,1:T(8,128)(2,1)S(1)}, bf16[256,256]{0,1:T(8,128)(2,1)S(1)}, u32[]{:S(2)}, u32[]{:S(2)}) collective-permute-start(bf16[256,256]{0,1:T(8,128)(2,1)S(1)} %slice_bitcast_fusion), channel_id=1, source_target_pairs={{0,1},{1,2},{2,3},{3,4},{4,5},{5,6},{6,7},{7,8},{8,9},{9,10},{10,1... | collective-permute-start | bytes 393224 | tf_op jit(solution)/shard_map/ppermute | solution.py:14
  95.3 1.2 copy-start.1
  95.3 1.3 copy-start.2
  95.3 1.4 copy-start.3
Sparse Core Ops, SparseCore 0:
  96.6 52.7 all-gather.1
where the time goes:
time: 186 us
  waiting for transfers between devices  120 us (65%)
  local copies, waits for them, and re-layouts  21.3 us (11%)
  between operations  13.6 us (7%)
  starting transfers between devices  13 us (7%)
  matrix products  10.2 us (5%)
  other arithmetic  7.53 us (4%)
    all_to_all x1, waiting for transfers between devices, per_device(): lax.all_to_all(raw_planes, 'tile', split_axis=0, concat_axis=1, tiled=True)  70.9 us
    all_gather x1, waiting for transfers between devices, fetch_bands(): shards = lax.all_gather(sections, 'tile', axis=0, tiled=True)  47.4 us
    all_to_all x1, starting transfers between devices, per_device(): lax.all_to_all(raw_planes, 'tile', split_axis=0, concat_axis=1, tiled=True)  10.5 us
    all_gather x1, local copies, waits for them, and re-layouts, fetch_bands(): shards = lax.all_gather(sections, 'tile', axis=0, tiled=True)  9 us
    gather x2, local copies, waits for them, and re-layouts, slice_band(): lax.dynamic_slice(shards, (which, row_start, zero_index), (1, BAND, colum...  7.83 us
  transfers between devices with their start and end apart: 3, of which 3 were waited for; matrix products, arithmetic and copies ran while one was open for 3% of the time, Pallas kernels for 0%

commit v1 on v0

--- a/solution.py
+++ b/solution.py
@@ -90,7 +90,8 @@
     zero_index = jnp.zeros((), jnp.int32)
     blank_bands = jnp.zeros((wanted, BAND, columns), sections.dtype)
     band_index = jnp.arange(BAND, dtype=jnp.int32)
-    shards = lax.all_gather(sections, "tile", axis=0, tiled=True)
+    sent = jnp.stack([sections] * lax.axis_size("tile"))
+    shards = jnp.concatenate(lax.all_to_all(sent, "tile", 0, 0), axis=0)
     held = shards.shape[0]
     inside = (section_ids >= 0) & (section_ids < held)
     clipped = jnp.clip(section_ids, 0, held - 1)

time: 186 us -> 273 us (1.47); the launches traced: 186 us -> 269 us
  waiting for transfers between devices: 120 us -> 206 us
  between operations: 13.6 us -> 0.21 us
  starting transfers between devices: 13 us -> 21.6 us
    all_to_all x0 -> x1, waiting for transfers between devices: none -> 133 us  [fetch_bands(): shards = jnp.concatenate(lax.all_to_all(sent, 'tile', 0, 0), axis=0)]
    all_gather x1 -> x0, waiting for transfers between devices: 47.4 us -> none  [fetch_bands(): shards = lax.all_gather(sections, 'tile', axis=0, tiled=True)]
    reshape x0 -> x1, local copies, waits for them, and re-layouts: none -> 9 us  [fetch_bands(): shards = jnp.concatenate(lax.all_to_all(sent, 'tile', 0, 0), axis=0)]
    all_gather x1 -> x0, local copies, waits for them, and re-layouts: 9 us -> none  [fetch_bands(): shards = lax.all_gather(sections, 'tile', axis=0, tiled=True)]
    all_to_all x0 -> x1, starting transfers between devices: none -> 8.8 us  [fetch_bands(): shards = jnp.concatenate(lax.all_to_all(sent, 'tile', 0, 0), axis=0)]
    another operation x0 -> x1, local copies, waits for them, and re-layouts: none -> 3.4 us  [fetch_bands(): sent = jnp.stack([sections] * lax.axis_size('tile'))]
  transfers between devices with their start and end apart: 3 -> 3, of which waited for: 3 -> 3; matrix products, arithmetic and copies ran while one was open for 3% -> 2% of each run, Pallas kernels for 0% -> 0%
where the time goes in v1:
time: 273 us; the launch traced here: 269 us
  waiting for transfers between devices  206 us (75%)
  local copies, waits for them, and re-layouts  24 us (9%)
  starting transfers between devices  21.6 us (8%)
  matrix products  10.2 us (4%)
  other arithmetic  7.53 us (3%)
    all_to_all x1, waiting for transfers between devices, fetch_bands(): shards = jnp.concatenate(lax.all_to_all(sent, 'tile', 0, 0), axis=0)  133 us
    all_to_all x1, waiting for transfers between devices, per_device(): lax.all_to_all(raw_planes, 'tile', split_axis=0, concat_axis=1, tiled=True)  71 us
    all_to_all x1, starting transfers between devices, per_device(): lax.all_to_all(raw_planes, 'tile', split_axis=0, concat_axis=1, tiled=True)  10.5 us
    reshape x1, local copies, waits for them, and re-layouts, fetch_bands(): shards = jnp.concatenate(lax.all_to_all(sent, 'tile', 0, 0), axis=0)  9 us
    all_to_all x1, starting transfers between devices, fetch_bands(): shards = jnp.concatenate(lax.all_to_all(sent, 'tile', 0, 0), axis=0)  8.8 us
    gather x2, local copies, waits for them, and re-layouts, slice_band(): lax.dynamic_slice(shards, (which, row_start, zero_index), (1, BAND, colum...  7.83 us
  transfers between devices with their start and end apart: 3, of which 3 were waited for; matrix products, arithmetic and copies ran while one was open for 2% of the time, Pallas kernels for 0%

profile of v1, /device:TPU:1, one launch (start us, length us, event | category | flops | bytes accessed | tf_op | source)
XLA Modules:
  0.0 269.4 jit_solution(12854243952144211217)
XLA Ops:
  0.0 0.0 copy-start
  0.0 10.5 %all-to-all-start = ((bf16[96,32,512]{2,1,0:T(8,128)(2,1)}), bf16[96,32,512]{2,1,0:T(8,128)(2,1)S(1)}, u32[]{:S(2)}, u32[]{:S(2)}) async-start(bf16[96,32,512]{2,1,0:T(8,128)(2,1)} %param.7), calls=%async_computation | async-start | bytes 6291456 | tf_op jit(solution)/shard_map/all_to_all | solution.py:140
  10.5 71.0 %all-to-all-done = bf16[96,32,512]{2,1,0:T(8,128)(2,1)S(1)} async-done(((bf16[96,32,512]{2,1,0:T(8,128)(2,1)}), bf16[96,32,512]{2,1,0:T(8,128)(2,1)S(1)}, u32[]{:S(2)}, u32[]{:S(2)}) %all-to-all-start) | async-done | bytes 3145760 | tf_op jit(solution)/shard_map/all_to_all | solution.py:140
  81.5 0.2 copy.48
  81.7 1.2 fusion
  82.9 0.7 copy.49
  83.6 0.8 fusion.15
  84.4 2.3 collective-permute-start
  86.8 1.9 collective-permute-done
  88.7 0.1 pad_maximum_fusion
  88.8 0.2 multiply_convert_fusion
  89.0 0.2 copy.51
  89.1 3.4 %stack.2 = bf16[16,3,256,256]{3,2,1,0:T(8,128)(2,1)} broadcast(bf16[3,256,256]{2,1,0:T(8,128)(2,1)S(1)} %copy.51), dimensions={1,2,3} | broadcast | bytes 6684672 | tf_op jit(solution)/shard_map/stack | solution.py:93
  92.5 0.0 copy-start.1
  92.5 0.0 copy-start.2
  92.5 0.0 copy-start.3
  92.5 8.8 %all-to-all-start.1 = ((bf16[16,3,256,256]{3,2,1,0:T(8,128)(2,1)}), bf16[16,3,256,256]{3,2,1,0:T(8,128)(2,1)}, u32[]{:S(2)}, u32[]{:S(2)}) async-start(bf16[16,3,256,256]{3,2,1,0:T(8,128)(2,1)} %stack.2), calls=%async_computation.1 | async-start | bytes 12582912 | tf_op jit(solution)/shard_map/all_to_all | solution.py:94
  101.3 0.0 copy-done.1
  101.3 0.1 copy.47
  101.4 0.0 copy-done.2
  101.4 0.1 copy.54
  101.5 0.0 copy-done.3
  101.5 0.2 convert_reduce_fusion
  101.7 0.1 select_reduce_fusion
  101.9 0.0 copy-done
  101.9 0.7 gather_fusion
  102.6 0.6 gather_fusion.2
  103.1 0.6 gather_fusion.3
  103.7 0.1 broadcast_select_fusion.1
  103.8 0.2 slice_reduce_fusion.1
  104.0 0.1 copy.56
  104.0 0.1 copy.55
  104.1 0.1 copy.53
  104.2 0.1 copy.52
  104.3 0.1 pad_add_fusion
  104.4 0.1 compare_and_fusion
  104.5 0.1 fusion.66
  104.6 0.1 fusion.59
  104.7 1.0 fusion.37
  105.7 1.0 multiply_convert_fusion.3
  106.7 0.1 broadcast_bitcast_fusion
  106.7 0.1 fusion.57
  106.8 133.0 %all-to-all-done.1 = bf16[16,3,256,256]{3,2,1,0:T(8,128)(2,1)} async-done(((bf16[16,3,256,256]{3,2,1,0:T(8,128)(2,1)}), bf16[16,3,256,256]{3,2,1,0:T(8,128)(2,1)}, u32[]{:S(2)}, u32[]{:S(2)}) %all-to-all-start.1) | async-done | bytes 6291488 | tf_op jit(solution)/shard_map/all_to_all | solution.py:94
  239.8 9.0 %copy.57 = bf16[48,256,256]{2,0,1:T(8,128)(2,1)} copy(bf16[48,256,256]{2,1,0:T(8,128)(2,1)} %bitcast.14) | data formatting | bytes 12582912 | tf_op jit(solution)/shard_map/reshape | solution.py:94
  248.8 7.5 %gather_fusion.1 = bf16[24,128,256]{2,0,1:T(8,128)(2,1)S(1)} fusion(bf16[48,256,256]{2,0,1:T(8,128)(2,1)} %copy.57, s32[24]{0:T(128)S(1)} %fusion.66), kind=kCustom, calls=%fused_computation.3 | custom fusion | bytes 3146016 | tf_op jit(solution)/shard_map/vmap()/gather | solution.py:100
  256.3 0.4 copy.58
  256.6 2.4 fusion.5
  259.1 1.0 convolution_convert_fusion
  260.1 0.8 fusion.10
  260.9 0.8 fusion.12
  261.7 0.8 subtract_bitcast_fusion
  262.6 0.9 add_bitcast_fusion
  263.4 1.2 fusion.21
  264.6 0.8 divide_convert_fusion.1
  265.4 0.6 fusion.50
  266.0 0.6 fusion.52
  266.6 0.6 fusion.17
  267.3 0.6 fusion.16
  267.9 1.5 fusion.18
  (9 shorter events, 0.1 us)
Async XLA Ops:
  0.0 101.9 %copy-start = (s32[64]{0:T(128)S(1)}, s32[64]{0:T(128)}, u32[]{:S(2)}) copy-start(s32[64]{0:T(128)} %param.10) | copy-start | bytes 772
  0.0 81.5 %all-to-all-start = ((bf16[96,32,512]{2,1,0:T(8,128)(2,1)}), bf16[96,32,512]{2,1,0:T(8,128)(2,1)S(1)}, u32[]{:S(2)}, u32[]{:S(2)}) async-start(bf16[96,32,512]{2,1,0:T(8,128)(2,1)} %param.7), calls=%async_computation | async-start | bytes 6291456 | tf_op jit(solution)/shard_map/all_to_all | solution.py:140
  84.4 4.2 %collective-permute-start = (bf16[256,256]{0,1:T(8,128)(2,1)S(1)}, bf16[256,256]{0,1:T(8,128)(2,1)S(1)}, u32[]{:S(2)}, u32[]{:S(2)}) collective-permute-start(bf16[256,256]{0,1:T(8,128)(2,1)S(1)} %slice_bitcast_fusion), channel_id=1, source_target_pairs={{0,1},{1,2},{2,3},{3,4},{4,5},{5,6},{6,7},{7,8},{8,9},{9,10},{10,1... | collective-permute-start | bytes 393224 | tf_op jit(solution)/shard_map/ppermute | solution.py:14
  92.5 8.8 %copy-start.1 = (s32[64,2]{0,1:T(2,128)S(1)}, s32[64,2]{0,1:T(2,128)}, u32[]{:S(2)}) copy-start(s32[64,2]{0,1:T(2,128)} %param.8) | copy-start | bytes 1540
  92.5 8.9 %copy-start.2 = (s32[64,2]{0,1:T(2,128)S(1)}, s32[64,2]{0,1:T(2,128)}, u32[]{:S(2)}) copy-start(s32[64,2]{0,1:T(2,128)} %param.9) | copy-start | bytes 1540
  92.5 9.0 %copy-start.3 = (s32[64,1]{0,1:T(1,128)S(1)}, s32[64,1]{0,1:T(1,128)}, u32[]{:S(2)}) copy-start(s32[64,1]{0,1:T(1,128)} %param.11) | copy-start | bytes 772
  92.5 147.3 %all-to-all-start.1 = ((bf16[16,3,256,256]{3,2,1,0:T(8,128)(2,1)}), bf16[16,3,256,256]{3,2,1,0:T(8,128)(2,1)}, u32[]{:S(2)}, u32[]{:S(2)}) async-start(bf16[16,3,256,256]{3,2,1,0:T(8,128)(2,1)} %stack.2), calls=%async_computation.1 | async-start | bytes 12582912 | tf_op jit(solution)/shard_map/all_to_all | solution.py:94
